TPU v7x, 256 devices: a whole 4x4x8 slice. The times are simulated.
256 devices in a mesh: row: 16 (over y, x_lo, core), col: 16 (over x_hi, z).
Axes of the slice: x: 4 (x_hi: 2, x_lo: 2; x = x_hi * 2 + x_lo), y: 4, z: 8, core: 2. Of those that a mesh axis runs over, the one named last changes fastest.
Arguments:
- frames: bfloat16 [2, 64, 128, 2048], P(None, None, 'row', 'col'), may hold values from -6 to 6
- state: bfloat16 [64, 128, 2048], P(None, 'row', 'col'), may hold values from -1 to 1
- input_weight: bfloat16 [9, 192, 64], replicated, may hold values from -0.25 to 0.25
- state_weight: bfloat16 [9, 192, 64], replicated, may hold values from -0.25 to 0.25
- cotangent: bfloat16 [64, 128, 2048], P(None, 'row', 'col'), may hold values from -6 to 6
Outputs:
- final_state: bfloat16 [64, 128, 2048], P(None, 'row', 'col')
- grad_state: float32 [64, 128, 2048], P(None, 'row', 'col')
- grad_input_weights: float32 [9, 192, 64], replicated
- grad_state_weights: float32 [9, 192, 64], replicated
All inputs are finite; a program needn't handle non-finite values.
Results may differ from a plain program's by a relative error of at most 0.0048.
Values may be sent and summed in bfloat16 or wider, within the bound.
A program may use at most 64 MiB of HBM per device.

v0:
```python
import functools

import jax
import jax.numpy as jnp
from jax import lax
from jax.experimental import pallas as pl
from jax.experimental.pallas import tpu as pltpu
from jax.sharding import PartitionSpec as P

HALO = 4


def padded_2(array, sides, width):
    for axis, dim in sides:
        devices, length = (lax.axis_size(axis), array.shape[dim])
        up = [(i, (i + 1) % devices) for i in range(devices - 1)]
        down = [(j, i) for i, j in up]
        last = lax.slice_in_dim(array, length - width, length, axis=dim)
        first = lax.slice_in_dim(array, 0, width, axis=dim)
        before = lax.ppermute(last, axis, up)
        after = lax.ppermute(first, axis, down)
        array = jnp.concatenate([before, array, after], axis=dim)
    return array


def shifted(flat, offsets, margin, length):
    return jnp.concatenate([flat[:, margin + off : margin + off + length] for off in offsets], 0)


def conv_flat(weights, flat, offsets, margin, length):
    taps, out_ch, in_ch = weights.shape
    stack = shifted(flat, offsets, margin, length)
    matrix = weights.transpose(1, 0, 2).reshape(out_ch, taps * in_ch)
    return jnp.dot(matrix, stack, preferred_element_type=jnp.float32)


def spread_flat(weights, flat, offsets, margin, length):
    taps, out_ch, in_ch = weights.shape
    stack = shifted(flat, [-off for off in offsets], margin, length)
    matrix = weights.transpose(2, 0, 1).reshape(in_ch, taps * out_ch)
    return jnp.dot(matrix, stack, preferred_element_type=jnp.float32)


def weight_flat(pre_grad, flat, offsets, margin, length):
    taps = len(offsets)
    stack = shifted(flat, offsets, margin, length)
    share = lax.dot_general(
        pre_grad, stack, (((1,), (1,)), ((), ())), preferred_element_type=jnp.float32
    )
    return share


def gates(from_input, from_state, previous, channels):
    update = jax.nn.sigmoid(from_input[:channels] + from_state[:channels])
    reset_gate = jax.nn.sigmoid(
        from_input[channels : 2 * channels] + from_state[channels : 2 * channels]
    )
    state_term = from_state[2 * channels :]
    candidate = jnp.tanh(from_input[2 * channels :] + reset_gate * state_term)
    new_state = ((1.0 - update) * candidate + update * previous.astype(jnp.float32)).astype(
        jnp.bfloat16
    )
    return new_state, (update, reset_gate, candidate, state_term)


def gate_grads(grad_state, saved, previous):
    update, reset_gate, candidate, state_term = saved
    grad_candidate = grad_state * (1.0 - update)
    grad_update = grad_state * (previous.astype(jnp.float32) - candidate)
    pre_update = grad_update * update * (1.0 - update)
    pre_candidate = grad_candidate * (1.0 - candidate * candidate)
    pre_reset = pre_candidate * state_term * reset_gate * (1.0 - reset_gate)
    pre_hidden = pre_candidate * reset_gate
    input_pre = jnp.concatenate([pre_update, pre_reset, pre_candidate], 0).astype(jnp.bfloat16)
    state_pre = jnp.concatenate([pre_update, pre_reset, pre_hidden], 0).astype(jnp.bfloat16)
    return (input_pre, state_pre, grad_state * update)


def reduce_kernel(rows, cols, x_ref, out_ref, got_row, summed, got_col, reduced, gathered, send_sem, recv_sem, own_sem):
    mesh_ids = pl.DeviceIdType.MESH
    me_row, me_col = lax.axis_index("row"), lax.axis_index("col")
    barrier = pltpu.get_barrier_semaphore()
    for axis, me, count in (("row", me_row, rows), ("col", me_col, cols)):

        def greet(distance, carry, axis=axis, me=me, count=count):
            peer = lax.rem(me + distance, count)
            pl.semaphore_signal(barrier, inc=1, device_id={axis: peer}, device_id_type=mesh_ids)
            return carry

        lax.fori_loop(1, count, greet, 0)
    pl.semaphore_wait(barrier, rows + cols - 2)
    piece = summed.shape[0] // cols

    def phase(index, axis, me, count, source, target):
        def copy_to(distance):
            peer = lax.rem(me + distance, count)
            return pltpu.make_async_remote_copy(
                src_ref=source(peer),
                dst_ref=target.at[me],
                send_sem=send_sem.at[index, distance],
                recv_sem=recv_sem.at[index, distance],
                device_id={axis: peer},
                device_id_type=mesh_ids,
            )

        def start(distance, carry):
            copy_to(distance).start()
            return carry

        def finish(distance, carry):
            copy_to(distance).wait()
            return carry

        lax.fori_loop(1, count, start, 0)
        own = pltpu.make_async_copy(source(me), target.at[me], own_sem.at[index])
        own.start()
        own.wait()
        lax.fori_loop(1, count, finish, 0)

    def total_of(buffer, count):
        return lax.fori_loop(1, count, lambda index, acc: acc + buffer[index], buffer[0])

    phase(0, "row", me_row, rows, lambda peer: x_ref.at[peer], got_row)
    summed[...] = total_of(got_row, rows)
    phase(
        1, "col", me_col, cols,
        lambda peer: summed.at[pl.ds(pl.multiple_of(peer * piece, piece), piece)], got_col,
    )
    reduced[...] = total_of(got_col, cols)
    phase(2, "col", me_col, cols, lambda peer: reduced, gathered)
    phase(3, "row", me_row, rows, lambda peer: gathered, out_ref)


def all_sum(parts):
    both = jnp.concatenate(parts, 0)
    rows, cols = lax.axis_size("row"), lax.axis_size("col")
    lanes = 128
    piece = -(-both.size // (rows * cols * lanes))
    piece = -(-piece // 8) * 8
    chunk = cols * piece * lanes
    padded_size = rows * chunk
    flat = jnp.pad(both.reshape(-1), (0, padded_size - both.size))
    count = max(rows, cols)
    out = pl.pallas_call(
        functools.partial(reduce_kernel, rows, cols),
        out_shape=jax.ShapeDtypeStruct((rows, cols, piece, lanes), jnp.float32),
        in_specs=[pl.BlockSpec(memory_space=pltpu.VMEM)],
        out_specs=pl.BlockSpec(memory_space=pltpu.VMEM),
        scratch_shapes=[
            pltpu.VMEM((rows, cols * piece, lanes), jnp.float32),
            pltpu.VMEM((cols * piece, lanes), jnp.float32),
            pltpu.VMEM((cols, piece, lanes), jnp.float32),
            pltpu.VMEM((piece, lanes), jnp.float32),
            pltpu.VMEM((cols, piece, lanes), jnp.float32),
            pltpu.SemaphoreType.DMA((4, count)),
            pltpu.SemaphoreType.DMA((4, count)),
            pltpu.SemaphoreType.DMA((4,)),
        ],
        compiler_params=pltpu.CompilerParams(collective_id=0, has_side_effects=True),
    )(flat.reshape(rows, cols * piece, lanes))
    return jnp.split(out.reshape(-1)[: both.size].reshape(both.shape), len(parts), 0)


def local(frames, state, input_weight, state_weight, cotangent):
    step_count = frames.shape[0]
    channels = state.shape[0]
    rows, cols = state.shape[1], state.shape[2]
    halo = HALO
    ext_rows, ext_cols = rows + 2 * halo, cols + 2 * halo
    length = ext_rows * ext_cols
    margin = ext_cols + 1
    offsets = [(k // 3 - 1) * ext_cols + (k % 3 - 1) for k in range(9)]

    fields = jnp.concatenate([frames.reshape(-1, rows, cols), state, cotangent], 0)
    fields = padded_2(fields, (("row", 1), ("col", 2)), halo).reshape(-1, length)
    frame_flat = [fields[t * frames.shape[1] : (t + 1) * frames.shape[1]] for t in range(step_count)]
    base = step_count * frames.shape[1]
    state_flat = fields[base : base + channels]
    cot_flat = fields[base + channels :]

    r = lax.broadcasted_iota(jnp.int32, (ext_rows, ext_cols), 0)
    c = lax.broadcasted_iota(jnp.int32, (ext_rows, ext_cols), 1)
    global_r = lax.axis_index("row") * rows + r - halo
    global_c = lax.axis_index("col") * cols + c - halo
    inside = (
        (global_r >= 0)
        & (global_r < rows * lax.axis_size("row"))
        & (global_c >= 0)
        & (global_c < cols * lax.axis_size("col"))
    ).reshape(1, length)
    own = ((r >= halo) & (r < halo + rows) & (c >= halo) & (c < halo + cols)).reshape(1, length)

    def pad(flat):
        return jnp.pad(flat, ((0, 0), (margin, margin)))

    records = []
    current = state_flat
    for step_index in range(step_count):
        frame_pad, state_pad = pad(frame_flat[step_index]), pad(current)
        from_input = conv_flat(input_weight, frame_pad, offsets, margin, length)
        from_state = conv_flat(state_weight, state_pad, offsets, margin, length)
        new_state, saved = gates(from_input, from_state, current, channels)
        records.append((frame_pad, state_pad, current, saved))
        current = jnp.where(inside, new_state, jnp.zeros_like(new_state))

    grad_state = cot_flat.astype(jnp.float32)
    input_pres, input_fields, state_pres, state_fields = [], [], [], []
    for step_index in reversed(range(step_count)):
        frame_pad, state_pad, previous, saved = records[step_index]
        input_pre, state_pre, direct = gate_grads(grad_state, saved, previous)
        input_pres.append(jnp.where(own, input_pre, jnp.zeros_like(input_pre)))
        state_pres.append(jnp.where(own, state_pre, jnp.zeros_like(state_pre)))
        input_fields.append(frame_pad)
        state_fields.append(state_pad)
        state_pre = jnp.where(inside, state_pre, jnp.zeros_like(state_pre))
        grad_state = direct + spread_flat(state_weight, pad(state_pre), offsets, margin, length)

    input_sum = sum(
        weight_flat(p, f, offsets, margin, length) for p, f in zip(input_pres, input_fields)
    )
    state_sum = sum(
        weight_flat(p, f, offsets, margin, length) for p, f in zip(state_pres, state_fields)
    )
    input_sum, state_sum = all_sum([input_sum, state_sum])
    taps, out_ch, in_ch = input_weight.shape
    input_sum = input_sum.reshape(out_ch, taps, in_ch).transpose(1, 0, 2)
    taps, out_ch, in_ch = state_weight.shape
    state_sum = state_sum.reshape(out_ch, taps, in_ch).transpose(1, 0, 2)
    loss_scale = (rows * lax.axis_size("row") * cols * lax.axis_size("col")) ** (-0.5)

    def crop(flat):
        return flat.reshape(-1, ext_rows, ext_cols)[:, halo : halo + rows, halo : halo + cols]

    return (crop(current), crop(grad_state), input_sum * loss_scale, state_sum * loss_scale)


def solution(mesh):
    in_specs = (P(None, None, "row", "col"), P(None, "row", "col"), P(), P(), P(None, "row", "col"))
    out_specs = (P(None, "row", "col"), P(None, "row", "col"), P(), P())
    return jax.shard_map(local, mesh=mesh, in_specs=in_specs, out_specs=out_specs, check_vma=False)
```

profile of v0, /device:TPU:1, one launch (start us, length us, event | category | flops | bytes accessed | tf_op | source)
XLA Modules:
  0.0 142.5 jit_solution(9346186776730122588)
XLA Ops:
  0.6 1.2 pad_maximum_fusion.9
  2.0 4.5 %collective-permute-start = (bf16[256,4,128]{2,1,0:T(4,128)(2,1)S(1)}, bf16[256,4,128]{2,1,0:T(4,128)(2,1)}, u32[]{:S(2)}, u32[]{:S(2)}) collective-permute-start(bf16[256,4,128]{2,1,0:T(4,128)(2,1)S(1)} %get-tuple-element.38), channel_id=1, source_target_pairs={{0,16},{16,32},{32,48},{48,64},{64,80},{80,96},{96,112},{112,128},... | collective-permute-start | bytes 786440 | tf_op jit(solution)/shard_map/ppermute | solution.py:20
  6.5 2.6 %collective-permute-start.1 = (bf16[256,4,128]{2,1,0:T(4,128)(2,1)S(1)}, bf16[256,4,128]{2,1,0:T(4,128)(2,1)S(1)}, u32[]{:S(2)}, u32[]{:S(2)}) collective-permute-start(bf16[256,4,128]{2,1,0:T(4,128)(2,1)S(1)} %get-tuple-element.39), channel_id=1, source_target_pairs={{16,0},{32,16},{48,32},{64,48},{80,64},{96,80},{112,96},{128,112},... | collective-permute-start | bytes 786440 | tf_op jit(solution)/shard_map/ppermute | solution.py:21
  9.3 0.5 collective-permute-done
  9.8 4.5 %collective-permute-done.1 = bf16[256,4,128]{2,1,0:T(4,128)(2,1)S(1)} collective-permute-done((bf16[256,4,128]{2,1,0:T(4,128)(2,1)S(1)}, bf16[256,4,128]{2,1,0:T(4,128)(2,1)S(1)}, u32[]{:S(2)}, u32[]{:S(2)}) %collective-permute-start.1) | collective-permute-done | bytes 262176 | tf_op jit(solution)/shard_map/ppermute | solution.py:21
  14.3 0.7 copy-done.20
  15.0 1.8 %pad_maximum_fusion.1 = bf16[256,16,128]{2,1,0:T(8,128)(2,1)S(1)} fusion(bf16[256,4,128]{2,1,0:T(4,128)(2,1)S(1)} %collective-permute-done.1, bf16[64,8,128]{2,1,0:T(8,128)(2,1)} %param.9, bf16[64,8,128]{2,1,0:T(8,128)(2,1)} %param.6, bf16[128,8,128]{2,1,0:T(8,128)(2,1)} %bitcast.54, bf16[256,4,128]{2,1,0:T(4,128)(2,1)} %collective-permute-done), kind=kLoop, calls=%fused_computation.11 | loop fusion | flops 5242880 | bytes 2097152 | tf_op jit(solution)/shard_map/concatenate | solution.py:22
  16.8 0.5 fusion.65
  17.3 0.9 copy.20
  18.3 0.9 copy.21
  19.2 1.3 collective-permute-start.3
  20.5 4.2 %collective-permute-start.2 = (bf16[256,16,4]{0,1,2:T(8,128)(2,1)S(1)}, bf16[256,16,4]{0,1,2:T(8,128)(2,1)S(1)}, u32[]{:S(2)}, u32[]{:S(2)}) collective-permute-start(bf16[256,16,4]{0,1,2:T(8,128)(2,1)S(1)} %copy.20), channel_id=1, source_target_pairs={{0,1},{1,2},{2,3},{3,4},{4,5},{5,6},{6,7},{7,8},{8,9},{9,10},{10,1... | collective-permute-start | bytes 98312 | tf_op jit(solution)/shard_map/ppermute | solution.py:20
  24.7 0.7 and.82
  25.4 0.7 and.78
  26.7 1.0 copy.22
  27.7 1.0 copy.23
  28.8 6.2 %pad_maximum_fusion = bf16[256,16,136]{2,1,0:T(8,128)(2,1)S(1)} fusion(bf16[256,16,4]{2,1,0:T(8,128)(2,1)S(1)} %copy.23, bf16[256,4,128]{2,1,0:T(4,128)(2,1)} %copy-done.20, bf16[64,8,128]{2,1,0:T(8,128)(2,1)S(1)} %copy-done.18, bf16[64,8,128]{2,1,0:T(8,128)(2,1)S(1)} %copy-done.19, bf16[128,8,128]{2,1,0:T(8,128)(2,1)S(1)} %bitcast.55, ...), kind=kLoop, calls=%fused_computation.8 | loop fusion | flops 7798784 | bytes 2228224 | tf_op jit(solution)/shard_map/concatenate | solution.py:22
  35.0 1.0 fusion.64
  36.0 1.7 %slice.276 = bf16[64,2176]{1,0:T(8,128)(2,1)S(1)} reshape(bf16[64,16,136]{2,1,0:T(8,128)(2,1)} %get-tuple-element.29) | data formatting | bytes 557056 | tf_op jit(solution)/shard_map/slice | solution.py:176
  37.7 0.7 slice.298
  38.4 0.7 slice.287
  39.1 1.4 reshape.135
  43.1 0.9 convolution_bitcast_fusion.2
  44.0 0.4 copy-done.9
  44.4 0.9 convolution_bitcast_fusion.1
  45.3 1.4 fusion.47
  47.9 0.9 convolution_bitcast_fusion
  50.0 0.9 convolution_bitcast_fusion.3
  51.6 0.9 fusion.46
  53.2 2.1 %fusion.6 = f32[192,576]{1,0:T(8,128)} fusion(bf16[576,2176]{1,0:T(8,128)(2,1)S(1)} %slice_dynamic-update-slice_fusion.16, pred[2176]{0:T(1024)(128)(4,1)S(1)} %copy-done.22, bf16[64,2176]{1,0:T(8,128)(2,1)S(1)} %get-tuple-element.28, bf16[64,2176]{1,0:T(8,128)(2,1)S(1)} %get-tuple-element.27, bf16[64,2176]{1,0:T(8,128)(2,1)S(1)} %fusion.23), kind=kOutput, calls=%fused_computation.23 | convolution fusion | flops 484220928 | bytes 3786880 | tf_op jit(solution)/shard_map/dot_general | solution.py:47
  55.2 1.9 %fusion.2 = f32[192,576]{1,0:T(8,128)} fusion(bf16[576,2176]{1,0:T(8,128)(2,1)S(1)} %slice_dynamic-update-slice_fusion.40, bf16[64,2176]{1,0:T(8,128)(2,1)S(1)} %get-tuple-element.18, pred[2176]{0:T(1024)(128)(4,1)S(1)} %copy-done.22, bf16[64,2176]{1,0:T(8,128)(2,1)S(1)} %get-tuple-element.27, bf16[64,2176]{1,0:T(8,128)(2,1)S(1)} %fusion.23), kind=kOutput, calls=%fused_computation.18 | convolution fusion | flops 484220928 | bytes 3786880 | tf_op jit(solution)/shard_map/dot_general | solution.py:47
  57.1 3.2 %reshape.129 = bf16[64,16,136]{2,1,0:T(8,128)(2,1)} reshape(bf16[64,2176]{1,0:T(8,128)(2,1)} %fusion.46) | data formatting | bytes 557056 | tf_op jit(solution)/shard_map/reshape | solution.py:232
  60.3 1.8 %slice.363 = bf16[64,8,128]{2,1,0:T(8,128)(2,1)} slice(bf16[64,16,136]{2,1,0:T(8,128)(2,1)} %reshape.129), slice={[0:64], [4:12], [4:132]} | slice | bytes 262144 | tf_op jit(solution)/shard_map/slice | solution.py:232
  65.4 2.4 %fusion.58 = (bf16[64,2176]{1,0:T(8,128)(2,1)S(1)}, f32[64,2176]{1,0:T(8,128)S(1)}, bf16[64,2176]{1,0:T(8,128)(2,1)S(1)}, f32[64,2176]{1,0:T(8,128)}) fusion(f32[64,2176]{1,0:T(8,128)S(1)} %copy-done.16, f32[64,2176]{1,0:T(8,128)S(1)} %copy-done.11, bf16[64,2176]{1,0:T(8,128)(2,1)S(1)} %slice.298, bf16[64,1728]{1,0:T(8,128)(2,1)S(1)} %reshape.130, ...), kind=kOutput, calls=%fused_computation.158 | convolution fusion | flops 483246080 | bytes 11919360 | tf_op jit(solution)/shard_map/dot_general | solution.py:41
  67.8 1.4 %multiply_convert_fusion.1 = (bf16[64,2176]{1,0:T(8,128)(2,1)S(1)}, bf16[64,2176]{1,0:T(8,128)(2,1)S(1)}) fusion(f32[64,2176]{1,0:T(8,128)S(1)} %get-tuple-element.17, f32[192,2176]{1,0:T(8,128)S(1)} %convolution_bitcast_fusion.1, f32[192,2176]{1,0:T(8,128)} %copy-done.2), kind=kLoop, calls=%fused_computation.88 | loop fusion | flops 1531904 | bytes 2785280 | tf_op jit(solution)/shard_map/convert.8
  69.8 1.1 convolution_add_fusion
  70.8 0.6 copy-done.8
  71.6 1.1 convolution_add_fusion.1
  72.7 0.4 reshape.132
  73.1 1.1 pad.30
  74.2 55.6 %shard_map.84 = f32[16,16,8,128]{3,2,1,0:T(8,128)} custom-call(f32[16,128,128]{2,1,0:T(8,128)} %bitcast.48), custom_call_target="tpu_custom_call" | custom-call | tf_op jit(solution)/shard_map/pallas_call | solution.py:144
  129.8 2.0 %slice_multiply_fusion = (f32[110592]{0:T(1024)}, f32[110592]{0:T(1024)S(1)}) fusion(f32[262144]{0:T(1024)} %bitcast.49), kind=kLoop, calls=%fused_computation.95 | loop fusion | flops 221184 | bytes 1769472 | tf_op jit(solution)/shard_map/mul | solution.py:234
  131.8 1.3 mul.142
  133.0 1.3 copy.26
  134.6 1.3 copy.25
  138.8 1.5 %fusion = f32[64,2176]{1,0:T(8,128)S(1)} fusion(bf16[64,1728]{1,0:T(8,128)(2,1)S(1)} %reshape.130, bf16[1728,2176]{1,0:T(8,128)(2,1)S(1)} %slice_dynamic-update-slice_fusion, f32[64,2176]{1,0:T(8,128)S(1)} %copy-done.17, f32[64,2176]{1,0:T(8,128)S(1)} %copy-done.12), kind=kOutput, calls=%fused_computation.5 | convolution fusion | flops 481574912 | bytes 9412608 | tf_op jit(solution)/shard_map/dot_general | solution.py:41
  140.2 1.4 reshape.131
  141.6 0.8 slice.365
  (119 shorter events, 14.1 us)
Async XLA Ops:
  0.6 42.2 %copy-start = (bf16[9,192,64]{1,2,0:T(8,128)(2,1)S(1)}, bf16[9,192,64]{1,2,0:T(8,128)(2,1)}, u32[]{:S(2)}) copy-start(bf16[9,192,64]{1,2,0:T(8,128)(2,1)} %param.7) | copy-start | bytes 663556
  2.0 7.8 %collective-permute-start = (bf16[256,4,128]{2,1,0:T(4,128)(2,1)S(1)}, bf16[256,4,128]{2,1,0:T(4,128)(2,1)}, u32[]{:S(2)}, u32[]{:S(2)}) collective-permute-start(bf16[256,4,128]{2,1,0:T(4,128)(2,1)S(1)} %get-tuple-element.38), channel_id=1, source_target_pairs={{0,16},{16,32},{32,48},{48,64},{64,80},{80,96},{96,112},{112,128},... | collective-permute-start | bytes 786440 | tf_op jit(solution)/shard_map/ppermute | solution.py:20
  6.5 7.8 %collective-permute-start.1 = (bf16[256,4,128]{2,1,0:T(4,128)(2,1)S(1)}, bf16[256,4,128]{2,1,0:T(4,128)(2,1)S(1)}, u32[]{:S(2)}, u32[]{:S(2)}) collective-permute-start(bf16[256,4,128]{2,1,0:T(4,128)(2,1)S(1)} %get-tuple-element.39), channel_id=1, source_target_pairs={{16,0},{32,16},{48,32},{64,48},{80,64},{96,80},{112,96},{128,112},... | collective-permute-start | bytes 786440 | tf_op jit(solution)/shard_map/ppermute | solution.py:21
  14.3 0.7 copy-start.20
  16.8 9.3 %copy-start.13 = (bf16[9,192,64]{1,2,0:T(8,128)(2,1)S(1)}, bf16[9,192,64]{1,2,0:T(8,128)(2,1)}, u32[]{:S(2)}) copy-start(bf16[9,192,64]{1,2,0:T(8,128)(2,1)} %param.8) | copy-start | bytes 663556
  18.2 10.5 %copy-start.15 = (bf16[2,64,8,128]{3,2,1,0:T(8,128)(2,1)S(1)}, bf16[2,64,8,128]{3,2,1,0:T(8,128)(2,1)}, u32[]{:S(2)}) copy-start(bf16[2,64,8,128]{3,2,1,0:T(8,128)(2,1)} %param.5) | copy-start | bytes 786436
  18.2 10.5 %copy-start.18 = (bf16[64,8,128]{2,1,0:T(8,128)(2,1)S(1)}, bf16[64,8,128]{2,1,0:T(8,128)(2,1)}, u32[]{:S(2)}) copy-start(bf16[64,8,128]{2,1,0:T(8,128)(2,1)} %param.9) | copy-start | bytes 393220
  18.2 10.5 %copy-start.19 = (bf16[64,8,128]{2,1,0:T(8,128)(2,1)S(1)}, bf16[64,8,128]{2,1,0:T(8,128)(2,1)}, u32[]{:S(2)}) copy-start(bf16[64,8,128]{2,1,0:T(8,128)(2,1)} %param.6) | copy-start | bytes 393220
  19.2 8.5 %collective-permute-start.3 = (bf16[256,16,4]{0,1,2:T(8,128)(2,1)S(1)}, bf16[256,16,4]{0,1,2:T(8,128)(2,1)S(1)}, u32[]{:S(2)}, u32[]{:S(2)}) collective-permute-start(bf16[256,16,4]{0,1,2:T(8,128)(2,1)S(1)} %copy.21), channel_id=1, source_target_pairs={{1,0},{2,1},{3,2},{4,3},{5,4},{6,5},{7,6},{8,7},{9,8},{10,9},{11,1... | collective-permute-start | bytes 98312 | tf_op jit(solution)/shard_map/ppermute | solution.py:21
  20.5 6.2 %collective-permute-start.2 = (bf16[256,16,4]{0,1,2:T(8,128)(2,1)S(1)}, bf16[256,16,4]{0,1,2:T(8,128)(2,1)S(1)}, u32[]{:S(2)}, u32[]{:S(2)}) collective-permute-start(bf16[256,16,4]{0,1,2:T(8,128)(2,1)S(1)} %copy.20), channel_id=1, source_target_pairs={{0,1},{1,2},{2,3},{3,4},{4,5},{5,6},{6,7},{7,8},{8,9},{9,10},{10,1... | collective-permute-start | bytes 98312 | tf_op jit(solution)/shard_map/ppermute | solution.py:20
  41.6 1.5 %copy-start.7 = (bf16[576,2176]{1,0:T(8,128)(2,1)}, bf16[576,2176]{1,0:T(8,128)(2,1)S(1)}, u32[]{:S(2)}) copy-start(bf16[576,2176]{1,0:T(8,128)(2,1)S(1)} %slice_dynamic-update-slice_fusion.32) | copy-start | bytes 7520260
  42.9 1.5 %copy-start.9 = (bf16[576,2176]{1,0:T(8,128)(2,1)}, bf16[576,2176]{1,0:T(8,128)(2,1)S(1)}, u32[]{:S(2)}) copy-start(bf16[576,2176]{1,0:T(8,128)(2,1)S(1)} %slice_dynamic-update-slice_fusion.24) | copy-start | bytes 7520260
  43.1 1.3 copy-start.14
  44.0 1.3 copy-start.2
  44.4 0.9 copy-start.21
  50.0 1.1 copy-start.3
  51.5 1.3 copy-start.5
  52.5 0.7 copy-start.22
  63.9 1.1 copy-start.4
  63.9 1.2 copy-start.6
  63.9 1.4 copy-start.11
  63.9 1.5 %copy-start.16 = (f32[64,2176]{1,0:T(8,128)S(1)}, f32[64,2176]{1,0:T(8,128)}, u32[]{:S(2)}) copy-start(f32[64,2176]{1,0:T(8,128)} %get-tuple-element.23) | copy-start | bytes 1671172
  67.8 1.9 %copy-start.10 = (bf16[576,2176]{1,0:T(8,128)(2,1)S(1)}, bf16[576,2176]{1,0:T(8,128)(2,1)}, u32[]{:S(2)}) copy-start(bf16[576,2176]{1,0:T(8,128)(2,1)} %copy-done.9) | copy-start | bytes 7520260
  67.8 1.9 %copy-start.24 = (f32[192,576]{1,0:T(8,128)S(1)}, f32[192,576]{1,0:T(8,128)}, u32[]{:S(2)}) copy-start(f32[192,576]{1,0:T(8,128)} %fusion.6) | copy-start | bytes 1327108
  69.8 1.7 %copy-start.8 = (bf16[576,2176]{1,0:T(8,128)(2,1)S(1)}, bf16[576,2176]{1,0:T(8,128)(2,1)}, u32[]{:S(2)}) copy-start(bf16[576,2176]{1,0:T(8,128)(2,1)} %copy-done.7) | copy-start | bytes 7520260
  69.8 1.8 %copy-start.23 = (f32[192,576]{1,0:T(8,128)S(1)}, f32[192,576]{1,0:T(8,128)}, u32[]{:S(2)}) copy-start(f32[192,576]{1,0:T(8,128)} %fusion.2) | copy-start | bytes 1327108
  137.6 1.1 copy-start.12
  137.6 1.2 copy-start.17
  138.8 3.7 %copy-start.1 = (bf16[9,192,64]{1,2,0:T(8,128)(2,1)S(1)}, bf16[9,192,64]{1,2,0:T(8,128)(2,1)}, u32[]{:S(2)}) copy-start(bf16[9,192,64]{1,2,0:T(8,128)(2,1)} %param.7) | copy-start | bytes 663556
where the time goes:
time: 143 us; the launch traced here: 142 us
  Pallas kernels  55.6 us (39%)
  local copies, waits for them, and re-layouts  37.2 us (26%)
  other arithmetic  17.2 us (12%)
  matrix products  13.4 us (9%)
  starting transfers between devices  12.6 us (9%)
  waiting for transfers between devices  5.05 us (4%)
    pallas_call x1, Pallas kernels, all_sum(): pl.pallas_call(functools.partial(reduce_kernel, rows, cols), out_shape=ja...  55.6 us
    unnamed x100, local copies, waits for them, and re-layouts  14.9 us
    ppermute x2, starting transfers between devices, padded_2(): before = lax.ppermute(last, axis, up)  8.68 us
    concatenate x2, other arithmetic, padded_2(): array = jnp.concatenate([before, array, after], axis=dim)  7.94 us
    dot_general x4, matrix products, weight_flat(): lax.dot_general(pre_grad, stack, (((1,), (1,)), ((), ())), preferred_elem...  6.07 us
    reshape x2, local copies, waits for them, and re-layouts, crop(): flat.reshape(-1, ext_rows, ext_cols)[:, halo:halo + rows, halo:halo + cols]  4.56 us
    ppermute x2, waiting for transfers between devices, padded_2(): after = lax.ppermute(first, axis, down)  4.52 us
    ppermute x2, starting transfers between devices, padded_2(): after = lax.ppermute(first, axis, down)  3.9 us
  transfers between devices with their start and end apart: 4, of which 2 were waited for; matrix products, arithmetic and copies ran while one was open for 2% of the time, Pallas kernels for 0%

commit v1 on v0

--- a/solution.py
+++ b/solution.py
@@ -21,6 +21,18 @@
         after = lax.ppermute(first, axis, down)
         array = jnp.concatenate([before, array, after], axis=dim)
     return array
+
+
+def aligned_halo(array, width):
+    array = padded_2(array, (("row", 1),), width)
+    devices = lax.axis_size("col")
+    up = [(i, i + 1) for i in range(devices - 1)]
+    down = [(j, i) for i, j in up]
+    left = lax.ppermute(array[:, :, -width:], "col", up)
+    right = lax.ppermute(array[:, :, :width], "col", down)
+    body = jnp.pad(jnp.concatenate([array, right], 2), ((0, 0), (1, 0), (0, 0)))
+    left = jnp.pad(left, ((0, 0), (0, 1), (0, 0)))
+    return jnp.concatenate([body, left], 2).reshape(array.shape[0], -1)
 
 
 def shifted(flat, offsets, margin, length):
@@ -172,7 +184,8 @@
     offsets = [(k // 3 - 1) * ext_cols + (k % 3 - 1) for k in range(9)]
 
     fields = jnp.concatenate([frames.reshape(-1, rows, cols), state, cotangent], 0)
-    fields = padded_2(fields, (("row", 1), ("col", 2)), halo).reshape(-1, length)
+    lead = ext_cols - halo
+    fields = aligned_halo(fields, halo)[:, lead : lead + length]
     frame_flat = [fields[t * frames.shape[1] : (t + 1) * frames.shape[1]] for t in range(step_count)]
     base = step_count * frames.shape[1]
     state_flat = fields[base : base + channels]

time: 143 us -> 162 us (1.13)
  local copies, waits for them, and re-layouts: 37.2 us -> 56.6 us
  matrix products: 13.4 us -> 20.1 us
  other arithmetic: 17.2 us -> 11.8 us
  Pallas kernels: 55.6 us -> 53 us
    concatenate x6, local copies, waits for them, and re-layouts: 1.16 us -> 14.3 us  [shifted(): jnp.concatenate([flat[:, margin + off:margin + off + length] for off in o...]
    slice x2 -> x4, local copies, waits for them, and re-layouts: 1.58 us -> 7.94 us  [the longest x1 5.62 us: shifted(): flat[:, margin + off:margin + off + length]]
    concatenate x2 -> x1, other arithmetic: 7.94 us -> 1.67 us  [padded_2(): array = jnp.concatenate([before, array, after], axis=dim)]
    ppermute x0 -> x2, starting transfers between devices: none -> 6.06 us  [the longest x1 4.78 us: aligned_halo(): left = lax.ppermute(array[:, :, -width:], 'col', up)]
    unnamed x100 -> x84, local copies, waits for them, and re-layouts: 14.9 us -> 20.8 us
    dot_general x4, matrix products: 3.52 us -> 8.76 us  [conv_flat(): return jnp.dot(matrix, stack, preferred_element_type=jnp.float32)]
    ppermute x2 -> x1, starting transfers between devices: 8.68 us -> 4.51 us  [padded_2(): before = lax.ppermute(last, axis, up)]
    concatenate x0 -> x2, other arithmetic: none -> 2.62 us  [the longest x1 2.52 us: aligned_halo(): body = jnp.pad(jnp.concatenate([array, right], 2), ((0, 0), (1, 0), (0, 0)))]
  transfers between devices with their start and end apart: 4 -> 4, of which waited for: 2 -> 2; matrix products, arithmetic and copies ran while one was open for 2% -> 5% of each run, Pallas kernels for 0% -> 0%
where the time goes in v1:
time: 162 us; the launch traced here: 161 us
  local copies, waits for them, and re-layouts  56.6 us (35%)
  Pallas kernels  53 us (33%)
  matrix products  20.1 us (12%)
  starting transfers between devices  12.5 us (8%)
  other arithmetic  11.8 us (7%)
  waiting for transfers between devices  5.72 us (4%)
    pallas_call x1, Pallas kernels, all_sum(): pl.pallas_call(functools.partial(reduce_kernel, rows, cols), out_shape=ja...  53 us
    unnamed x84, local copies, waits for them, and re-layouts  20.8 us
    concatenate x6, local copies, waits for them, and re-layouts, shifted(): jnp.concatenate([flat[:, margin + off:margin + off + length] for off in o...  14.3 us
    dot_general x4, matrix products, conv_flat(): return jnp.dot(matrix, stack, preferred_element_type=jnp.float32)  8.76 us
    dot_general x4, matrix products, weight_flat(): lax.dot_general(pre_grad, stack, (((1,), (1,)), ((), ())), preferred_elem...  7.55 us
    slice x1, local copies, waits for them, and re-layouts, shifted(): flat[:, margin + off:margin + off + length]  5.62 us
    ppermute x1, starting transfers between devices, aligned_halo(): left = lax.ppermute(array[:, :, -width:], 'col', up)  4.78 us
    ppermute x1, waiting for transfers between devices, padded_2(): after = lax.ppermute(first, axis, down)  4.51 us
  transfers between devices with their start and end apart: 4, of which 2 were waited for; matrix products, arithmetic and copies ran while one was open for 5% of the time, Pallas kernels for 0%

profile of v1, /device:TPU:1, one launch (start us, length us, event | category | flops | bytes accessed | tf_op | source)
XLA Modules:
  0.0 161.1 jit_solution(11653937649431729904)
XLA Ops:
  0.6 1.2 pad_maximum_fusion.9
  2.0 4.5 %collective-permute-start = (bf16[256,4,128]{2,1,0:T(4,128)(2,1)S(1)}, bf16[256,4,128]{2,1,0:T(4,128)(2,1)S(1)}, u32[]{:S(2)}, u32[]{:S(2)}) collective-permute-start(bf16[256,4,128]{2,1,0:T(4,128)(2,1)S(1)} %get-tuple-element.54), channel_id=1, source_target_pairs={{0,16},{16,32},{32,48},{48,64},{64,80},{80,96},{96,112},{112,128},... | collective-permute-start | bytes 786440 | tf_op jit(solution)/shard_map/ppermute | solution.py:20
  6.5 1.9 %collective-permute-start.1 = (bf16[256,4,128]{2,1,0:T(4,128)(2,1)S(1)}, bf16[256,4,128]{2,1,0:T(4,128)(2,1)S(1)}, u32[]{:S(2)}, u32[]{:S(2)}) collective-permute-start(bf16[256,4,128]{2,1,0:T(4,128)(2,1)S(1)} %get-tuple-element.55), channel_id=1, source_target_pairs={{16,0},{32,16},{48,32},{64,48},{80,64},{96,80},{112,96},{128,112},... | collective-permute-start | bytes 786440 | tf_op jit(solution)/shard_map/ppermute | solution.py:21
  8.6 1.2 collective-permute-done
  9.8 4.5 %collective-permute-done.1 = bf16[256,4,128]{2,1,0:T(4,128)(2,1)S(1)} collective-permute-done((bf16[256,4,128]{2,1,0:T(4,128)(2,1)S(1)}, bf16[256,4,128]{2,1,0:T(4,128)(2,1)S(1)}, u32[]{:S(2)}, u32[]{:S(2)}) %collective-permute-start.1) | collective-permute-done | bytes 262176 | tf_op jit(solution)/shard_map/ppermute | solution.py:21
  15.1 1.7 %pad_maximum_fusion.1 = bf16[256,16,128]{2,1,0:T(8,128)(2,1)S(1)} fusion(bf16[256,4,128]{2,1,0:T(4,128)(2,1)S(1)} %collective-permute-done.1, bf16[64,8,128]{2,1,0:T(8,128)(2,1)} %param.9, bf16[64,8,128]{2,1,0:T(8,128)(2,1)} %param.6, bf16[128,8,128]{2,1,0:T(8,128)(2,1)} %bitcast.56, bf16[256,4,128]{2,1,0:T(4,128)(2,1)S(1)} %collective-permute-done), kind=kLoop, calls=%fused_computation.16 | loop fusion | flops 5242880 | bytes 2097152 | tf_op jit(solution)/shard_map/concatenate | solution.py:22
  17.2 0.9 copy.23
  18.1 1.3 collective-permute-start.2
  19.9 1.0 reshape.127
  21.0 0.9 copy.25
  21.9 4.8 %collective-permute-start.3 = (bf16[256,16,4]{0,1,2:T(8,128)(2,1)S(1)}, bf16[256,16,4]{0,1,2:T(8,128)(2,1)}, u32[]{:S(2)}, u32[]{:S(2)}) collective-permute-start(bf16[256,16,4]{0,1,2:T(8,128)(2,1)S(1)} %copy.25), channel_id=1, source_target_pairs={{0,1},{1,2},{2,3},{3,4},{4,5},{5,6},{6,7},{7,8},{8,9},{9,10},{10,1... | collective-permute-start | bytes 98312 | tf_op jit(solution)/shard_map/ppermute | solution.py:31
  26.7 1.0 copy.24
  27.7 2.5 %pad_maximum_fusion = bf16[256,16,132]{2,1,0:T(8,128)(2,1)S(1)} fusion(bf16[256,16,4]{2,1,0:T(8,128)(2,1)S(1)} %copy.24, bf16[256,4,128]{2,1,0:T(4,128)(2,1)} %copy-done.20, bf16[64,8,128]{2,1,0:T(8,128)(2,1)} %param.9, bf16[64,8,128]{2,1,0:T(8,128)(2,1)} %param.6, bf16[128,8,128]{2,1,0:T(8,128)(2,1)} %bitcast.57, bf16[256,4,128]{2,1,0:T(4,128)(2,1)} %copy-done.19), kind=kLoop, calls=%fused_computation.12 | loop fusion | flops 6488064 | bytes 2162688 | tf_op jit(solution)/shard_map/concatenate | solution.py:33
  30.2 2.0 %copy.35 = bf16[256,16,132]{0,2,1:T(8,128)(2,1)S(1)} copy(bf16[256,16,132]{2,1,0:T(8,128)(2,1)S(1)} %pad_maximum_fusion) | data formatting | bytes 2162688
  34.1 1.0 copy.34
  35.1 0.8 slice_dynamic-update-slice_fusion.31
  36.0 0.8 slice_dynamic-update-slice_fusion.30
  36.8 0.9 slice_dynamic-update-slice_fusion.29
  37.7 0.9 slice_dynamic-update-slice_fusion.28
  40.1 0.8 slice_dynamic-update-slice_fusion.26
  40.9 0.9 slice_dynamic-update-slice_fusion.25
  41.8 0.9 slice_dynamic-update-slice_fusion.24
  42.7 5.6 %pad_slice_fusion = (bf16[64,2176]{0,1:T(8,128)(2,1)}, bf16[64,2176]{0,1:T(8,128)(2,1)}, bf16[64,2176]{0,1:T(8,128)(2,1)}, bf16[64,2176]{0,1:T(8,128)(2,1)}, bf1...) fusion(bf16[64,2176]{0,1:T(8,128)(2,1)S(1)} %get-tuple-element., ...), kind=kLoop, calls=%fused_computation.107 | loop fusion | bytes 5013504 | tf_op jit(solution)/shard_map/slice | solution.py:39
  48.3 5.6 %concatenate.58 = bf16[576,2176]{0,1:T(8,128)(2,1)S(1)} concatenate(bf16[64,2176]{0,1:T(8,128)(2,1)} %get-tuple-element.53, bf16[64,2176]{0,1:T(8,128)(2,1)} %get-tuple-element.47, bf16[64,2176]{0,1:T(8,128)(2,1)} %get-tuple-element.48, bf16[64,2176]{0,1:T(8,128)(2,1)} %get-tuple-element.49, bf16[64,2176]{0,1:T(8,128)(2,1)} %copy-done.11, bf16[64,2176]{0,1:T(8,128)(2,1)} %get-tuple-element.50, ...), dimensions={0} | concatenate | bytes 5013504 | tf_op jit(solution)/shard_map/concatenate | solution.py:39
  54.0 2.3 %convolution_bitcast_fusion = f32[192,2176]{1,0:T(8,128)} fusion(bf16[576,2176]{0,1:T(8,128)(2,1)S(1)} %concatenate.58, bf16[192,576]{0,1:T(8,128)(2,1)S(1)} %bitcast.46), kind=kOutput, calls=%fused_computation | convolution fusion | flops 481296384 | bytes 4399104 | tf_op jit(solution)/shard_map/dot_general | solution.py:46
  56.3 7.1 %concatenate.57 = bf16[576,2176]{0,1:T(8,128)(2,1)} concatenate(bf16[64,2176]{0,1:T(8,128)(2,1)} %get-tuple-element.57, bf16[64,2176]{0,1:T(8,128)(2,1)} %get-tuple-element.63, bf16[64,2176]{0,1:T(8,128)(2,1)} %get-tuple-element.62, bf16[64,2176]{0,1:T(8,128)(2,1)} %get-tuple-element.61, bf16[64,2176]{0,1:T(8,128)(2,1)} %copy-done.10, bf16[64,2176]{0,1:T(8,128)(2,1)} %get-tuple-element.60, ...), dimensions={0} | concatenate | bytes 5013504 | tf_op jit(solution)/shard_map/concatenate | solution.py:39
  63.4 2.9 %convolution_bitcast_fusion.1 = f32[192,2176]{1,0:T(8,128)S(1)} fusion(bf16[576,2176]{0,1:T(8,128)(2,1)} %concatenate.57, bf16[192,576]{0,1:T(8,128)(2,1)S(1)} %bitcast.45), kind=kOutput, calls=%fused_computation.1 | convolution fusion | flops 481296384 | bytes 4399104 | tf_op jit(solution)/shard_map/dot_general | solution.py:46
  66.3 2.7 %convolution_bitcast_fusion.3 = f32[192,2176]{1,0:T(8,128)S(1)} fusion(bf16[576,2176]{1,0:T(8,128)(2,1)} %slice_dynamic-update-slice_fusion.24, bf16[192,576]{0,1:T(8,128)(2,1)S(1)} %bitcast.53), kind=kOutput, calls=%fused_computation.3 | convolution fusion | flops 481296384 | bytes 4399104 | tf_op jit(solution)/shard_map/dot_general | solution.py:46
  69.0 1.4 fusion.50
  71.6 0.9 convolution_bitcast_fusion.2
  73.9 1.8 %fusion.9 = f32[192,576]{1,0:T(8,128)} fusion(bf16[576,2176]{1,0:T(8,128)(2,1)S(1)} %slice_dynamic-update-slice_fusion.16, pred[2176]{0:T(1024)(128)(4,1)S(1)} %and.82, bf16[64,2176]{1,0:T(8,128)(2,1)S(1)} %get-tuple-element.28, bf16[64,2176]{1,0:T(8,128)(2,1)S(1)} %get-tuple-element.27, bf16[64,2176]{1,0:T(8,128)(2,1)S(1)} %fusion.25), kind=kOutput, calls=%fused_computation.28 | convolution fusion | flops 484220928 | bytes 3786880 | tf_op jit(solution)/shard_map/dot_general | solution.py:59
  75.8 1.7 %fusion.5 = f32[192,576]{1,0:T(8,128)} fusion(bf16[576,2176]{0,1:T(8,128)(2,1)S(1)} %copy-done.4, bf16[64,2176]{1,0:T(8,128)(2,1)S(1)} %get-tuple-element.18, pred[2176]{0:T(1024)(128)(4,1)S(1)} %and.82, bf16[64,2176]{1,0:T(8,128)(2,1)S(1)} %get-tuple-element.27, bf16[64,2176]{1,0:T(8,128)(2,1)S(1)} %fusion.25), kind=kOutput, calls=%fused_computation.23 | convolution fusion | flops 484220928 | bytes 3786880 | tf_op jit(solution)/shard_map/dot_general | solution.py:59
  77.4 2.2 %reshape.126 = bf16[64,16,136]{2,1,0:T(8,128)(2,1)} reshape(bf16[64,2176]{1,0:T(8,128)(2,1)S(1)} %fusion.49) | data formatting | bytes 557056 | tf_op jit(solution)/shard_map/reshape | solution.py:245
  79.6 1.8 %slice.355 = bf16[64,8,128]{2,1,0:T(8,128)(2,1)} slice(bf16[64,16,136]{2,1,0:T(8,128)(2,1)} %reshape.126), slice={[0:64], [4:12], [4:132]} | slice | bytes 262144 | tf_op jit(solution)/shard_map/slice | solution.py:245
  84.7 2.3 %fusion.61 = (bf16[64,2176]{1,0:T(8,128)(2,1)S(1)}, f32[64,2176]{1,0:T(8,128)S(1)}, bf16[64,2176]{1,0:T(8,128)(2,1)S(1)}, f32[64,2176]{1,0:T(8,128)}) fusion(f32[64,2176]{1,0:T(8,128)S(1)} %copy-done.17, f32[64,2176]{1,0:T(8,128)S(1)} %copy-done.8, bf16[64,2176]{1,0:T(8,128)(2,1)S(1)} %copy.33, bf16[64,1728]{1,0:T(8,128)(2,1)S(1)} %copy-done.12, ...), kind=kOutput, calls=%fused_computation.162 | convolution fusion | flops 483385344 | bytes 11640832 | tf_op jit(solution)/shard_map/dot_general | solution.py:53
  87.1 1.3 multiply_convert_fusion.1
  88.6 3.2 %convolution_add_fusion = f32[192,576]{1,0:T(8,128)S(1)} fusion(f32[192,576]{1,0:T(8,128)S(1)} %copy-done.21, bf16[576,2176]{1,0:T(8,128)(2,1)} %slice_dynamic-update-slice_fusion.24, pred[2176]{0:T(1024)(128)(4,1)S(1)} %and.82, bf16[64,2176]{1,0:T(8,128)(2,1)S(1)} %get-tuple-element.26, bf16[64,2176]{1,0:T(8,128)(2,1)S(1)} %get-tuple-element.25, ...), kind=kOutput, calls=%fused_computation.13 | convolution fusion | flops 484331520 | bytes 4229248 | tf_op jit(solution)/shard_map/dot_general | solution.py:59
  91.8 0.9 convolution_add_fusion.1
  93.2 1.0 pad.40
  94.2 53.0 %shard_map.84 = f32[16,16,8,128]{3,2,1,0:T(8,128)} custom-call(f32[16,128,128]{2,1,0:T(8,128)} %bitcast.50), custom_call_target="tpu_custom_call" | custom-call | tf_op jit(solution)/shard_map/pallas_call | solution.py:156
  147.2 2.1 %slice_multiply_fusion = (f32[110592]{0:T(1024)}, f32[110592]{0:T(1024)}) fusion(f32[262144]{0:T(1024)} %bitcast.51), kind=kLoop, calls=%fused_computation.101 | loop fusion | flops 221184 | bytes 1769472 | tf_op jit(solution)/shard_map/mul | solution.py:247
  149.3 1.3 mul.142
  150.6 1.3 copy.32
  151.9 1.3 mul.139
  153.2 1.3 copy.31
  157.4 1.5 fusion
  158.8 1.4 reshape.128
  160.2 0.8 slice.357
  (100 shorter events, 14.6 us)
Async XLA Ops:
  0.6 53.3 %copy-start = (bf16[9,192,64]{1,2,0:T(8,128)(2,1)S(1)}, bf16[9,192,64]{1,2,0:T(8,128)(2,1)}, u32[]{:S(2)}) copy-start(bf16[9,192,64]{1,2,0:T(8,128)(2,1)} %param.7) | copy-start | bytes 663556
  2.0 7.8 %collective-permute-start = (bf16[256,4,128]{2,1,0:T(4,128)(2,1)S(1)}, bf16[256,4,128]{2,1,0:T(4,128)(2,1)S(1)}, u32[]{:S(2)}, u32[]{:S(2)}) collective-permute-start(bf16[256,4,128]{2,1,0:T(4,128)(2,1)S(1)} %get-tuple-element.54), channel_id=1, source_target_pairs={{0,16},{16,32},{32,48},{48,64},{64,80},{80,96},{96,112},{112,128},... | collective-permute-start | bytes 786440 | tf_op jit(solution)/shard_map/ppermute | solution.py:20
  6.5 7.8 %collective-permute-start.1 = (bf16[256,4,128]{2,1,0:T(4,128)(2,1)S(1)}, bf16[256,4,128]{2,1,0:T(4,128)(2,1)S(1)}, u32[]{:S(2)}, u32[]{:S(2)}) collective-permute-start(bf16[256,4,128]{2,1,0:T(4,128)(2,1)S(1)} %get-tuple-element.55), channel_id=1, source_target_pairs={{16,0},{32,16},{48,32},{64,48},{80,64},{96,80},{112,96},{128,112},... | collective-permute-start | bytes 786440 | tf_op jit(solution)/shard_map/ppermute | solution.py:21
  9.8 4.5 %copy-start.19 = (bf16[256,4,128]{2,1,0:T(4,128)(2,1)}, bf16[256,4,128]{2,1,0:T(4,128)(2,1)S(1)}, u32[]{:S(2)}) copy-start(bf16[256,4,128]{2,1,0:T(4,128)(2,1)S(1)} %collective-permute-done) | copy-start | bytes 786436
  14.3 0.7 copy-start.20
  16.7 3.0 %copy-start.15 = (bf16[9,192,64]{1,2,0:T(8,128)(2,1)S(1)}, bf16[9,192,64]{1,2,0:T(8,128)(2,1)}, u32[]{:S(2)}) copy-start(bf16[9,192,64]{1,2,0:T(8,128)(2,1)} %param.8) | copy-start | bytes 663556
  18.1 8.6 %collective-permute-start.2 = (bf16[256,16,4]{0,1,2:T(8,128)(2,1)S(1)}, bf16[256,16,4]{0,1,2:T(8,128)(2,1)S(1)}, u32[]{:S(2)}, u32[]{:S(2)}) collective-permute-start(bf16[256,16,4]{0,1,2:T(8,128)(2,1)S(1)} %copy.23), channel_id=1, source_target_pairs={{1,0},{2,1},{3,2},{4,3},{5,4},{6,5},{7,6},{8,7},{9,8},{10,9},{11,1... | collective-permute-start | bytes 98312 | tf_op jit(solution)/shard_map/ppermute | solution.py:32
  21.9 10.3 %collective-permute-start.3 = (bf16[256,16,4]{0,1,2:T(8,128)(2,1)S(1)}, bf16[256,16,4]{0,1,2:T(8,128)(2,1)}, u32[]{:S(2)}, u32[]{:S(2)}) collective-permute-start(bf16[256,16,4]{0,1,2:T(8,128)(2,1)S(1)} %copy.25), channel_id=1, source_target_pairs={{0,1},{1,2},{2,3},{3,4},{4,5},{5,6},{6,7},{7,8},{8,9},{9,10},{10,1... | collective-permute-start | bytes 98312 | tf_op jit(solution)/shard_map/ppermute | solution.py:31
  33.9 8.8 %copy-start.10 = (bf16[64,2176]{0,1:T(8,128)(2,1)}, bf16[64,2176]{0,1:T(8,128)(2,1)S(1)}, u32[]{:S(2)}) copy-start(bf16[64,2176]{0,1:T(8,128)(2,1)S(1)} %get-tuple-element.30) | copy-start | bytes 835588
  33.9 8.8 %copy-start.11 = (bf16[64,2176]{0,1:T(8,128)(2,1)}, bf16[64,2176]{0,1:T(8,128)(2,1)S(1)}, u32[]{:S(2)}) copy-start(bf16[64,2176]{0,1:T(8,128)(2,1)S(1)} %get-tuple-element.33) | copy-start | bytes 835588
  54.0 9.4 %copy-start.2 = (bf16[576,2176]{0,1:T(8,128)(2,1)}, bf16[576,2176]{0,1:T(8,128)(2,1)S(1)}, u32[]{:S(2)}) copy-start(bf16[576,2176]{0,1:T(8,128)(2,1)S(1)} %concatenate.58) | copy-start | bytes 7520260
  63.3 2.9 %copy-start.16 = (bf16[9,192,64]{1,2,0:T(8,128)(2,1)S(1)}, bf16[9,192,64]{1,2,0:T(8,128)(2,1)}, u32[]{:S(2)}) copy-start(bf16[9,192,64]{1,2,0:T(8,128)(2,1)} %param.8) | copy-start | bytes 663556
  66.3 2.7 %copy-start.5 = (f32[192,2176]{1,0:T(8,128)S(1)}, f32[192,2176]{1,0:T(8,128)}, u32[]{:S(2)}) copy-start(f32[192,2176]{1,0:T(8,128)} %convolution_bitcast_fusion) | copy-start | bytes 5013508
  71.6 1.0 copy-start.13
  73.0 0.8 copy-start.6
  73.9 1.8 %copy-start.4 = (bf16[576,2176]{0,1:T(8,128)(2,1)S(1)}, bf16[576,2176]{0,1:T(8,128)(2,1)}, u32[]{:S(2)}) copy-start(bf16[576,2176]{0,1:T(8,128)(2,1)} %concatenate.57) | copy-start | bytes 7520260
  83.2 1.1 copy-start.7
  83.2 1.2 copy-start.8
  83.2 1.3 copy-start.12
  83.2 1.3 copy-start.14
  83.2 1.5 copy-start.17
  87.1 1.5 copy-start.21
  88.6 3.2 %copy-start.3 = (bf16[576,2176]{0,1:T(8,128)(2,1)S(1)}, bf16[576,2176]{0,1:T(8,128)(2,1)}, u32[]{:S(2)}) copy-start(bf16[576,2176]{0,1:T(8,128)(2,1)} %copy-done.2) | copy-start | bytes 7520260
  88.6 3.2 %copy-start.22 = (f32[192,576]{1,0:T(8,128)S(1)}, f32[192,576]{1,0:T(8,128)}, u32[]{:S(2)}) copy-start(f32[192,576]{1,0:T(8,128)} %fusion.5) | copy-start | bytes 1327108
  156.1 1.1 copy-start.9
  156.2 1.2 copy-start.18
  157.4 3.7 %copy-start.1 = (bf16[9,192,64]{1,2,0:T(8,128)(2,1)S(1)}, bf16[9,192,64]{1,2,0:T(8,128)(2,1)}, u32[]{:S(2)}) copy-start(bf16[9,192,64]{1,2,0:T(8,128)(2,1)} %param.7) | copy-start | bytes 663556

commit v2 on v0

--- a/solution.py
+++ b/solution.py
@@ -124,7 +124,7 @@
     summed[...] = total_of(got_row, rows)
     phase(
         1, "col", me_col, cols,
-        lambda peer: summed.at[pl.ds(pl.multiple_of(peer * piece, piece), piece)], got_col,
+        lambda peer: summed.at[pl.ds(peer * piece, piece)], got_col,
     )
     reduced[...] = total_of(got_col, cols)
     phase(2, "col", me_col, cols, lambda peer: reduced, gathered)
@@ -136,7 +136,6 @@
     rows, cols = lax.axis_size("row"), lax.axis_size("col")
     lanes = 128
     piece = -(-both.size // (rows * cols * lanes))
-    piece = -(-piece // 8) * 8
     chunk = cols * piece * lanes
     padded_size = rows * chunk
     flat = jnp.pad(both.reshape(-1), (0, padded_size - both.size))

time: 143 us -> 141 us (0.986)
  Pallas kernels: 55.6 us -> 53.5 us
    pallas_call x1, Pallas kernels: 55.6 us -> 53.5 us  [all_sum(): pl.pallas_call(functools.partial(reduce_kernel, rows, cols), out_shape=ja...]
    unnamed x100 -> x96, local copies, waits for them, and re-layouts: 14.9 us -> 14.7 us
  transfers between devices with their start and end apart: 4 -> 4, of which waited for: 2 -> 3; matrix products, arithmetic and copies ran while one was open for 2% -> 1% of each run, Pallas kernels for 0% -> 0%
where the time goes in v2:
time: 141 us; the launch traced here: 140 us
  Pallas kernels  53.5 us (38%)
  local copies, waits for them, and re-layouts  38.1 us (27%)
  other arithmetic  16 us (11%)
  matrix products  13.4 us (10%)
  starting transfers between devices  11.9 us (8%)
  waiting for transfers between devices  5.85 us (4%)
  between operations  1.42 us (1%)
    pallas_call x1, Pallas kernels, all_sum(): pl.pallas_call(functools.partial(reduce_kernel, rows, cols), out_shape=ja...  53.5 us
    unnamed x96, local copies, waits for them, and re-layouts  14.7 us
    ppermute x2, starting transfers between devices, padded_2(): before = lax.ppermute(last, axis, up)  8.68 us
    concatenate x2, other arithmetic, padded_2(): array = jnp.concatenate([before, array, after], axis=dim)  7.86 us
    dot_general x4, matrix products, weight_flat(): lax.dot_general(pre_grad, stack, (((1,), (1,)), ((), ())), preferred_elem...  6.07 us
    reshape x2, local copies, waits for them, and re-layouts, crop(): flat.reshape(-1, ext_rows, ext_cols)[:, halo:halo + rows, halo:halo + cols]  4.58 us
    ppermute x2, waiting for transfers between devices, padded_2(): after = lax.ppermute(first, axis, down)  4.52 us
    dot_general x2, matrix products, spread_flat(): return jnp.dot(matrix, stack, preferred_element_type=jnp.float32)  3.82 us
  transfers between devices with their start and end apart: 4, of which 3 were waited for; matrix products, arithmetic and copies ran while one was open for 1% of the time, Pallas kernels for 0%

profile of v2, /device:TPU:1, one launch (start us, length us, event | category | flops | bytes accessed | tf_op | source)
XLA Modules:
  0.0 140.2 jit_solution(4585675072740457108)
XLA Ops:
  0.6 1.2 pad_maximum_fusion.9
  2.0 4.5 %collective-permute-start = (bf16[256,4,128]{2,1,0:T(4,128)(2,1)S(1)}, bf16[256,4,128]{2,1,0:T(4,128)(2,1)S(1)}, u32[]{:S(2)}, u32[]{:S(2)}) collective-permute-start(bf16[256,4,128]{2,1,0:T(4,128)(2,1)S(1)} %get-tuple-element.38), channel_id=1, source_target_pairs={{0,16},{16,32},{32,48},{48,64},{64,80},{80,96},{96,112},{112,128},... | collective-permute-start | bytes 786440 | tf_op jit(solution)/shard_map/ppermute | solution.py:20
  6.5 1.9 %collective-permute-start.1 = (bf16[256,4,128]{2,1,0:T(4,128)(2,1)S(1)}, bf16[256,4,128]{2,1,0:T(4,128)(2,1)S(1)}, u32[]{:S(2)}, u32[]{:S(2)}) collective-permute-start(bf16[256,4,128]{2,1,0:T(4,128)(2,1)S(1)} %get-tuple-element.39), channel_id=1, source_target_pairs={{16,0},{32,16},{48,32},{64,48},{80,64},{96,80},{112,96},{128,112},... | collective-permute-start | bytes 786440 | tf_op jit(solution)/shard_map/ppermute | solution.py:21
  8.6 1.2 collective-permute-done
  9.8 4.5 %collective-permute-done.1 = bf16[256,4,128]{2,1,0:T(4,128)(2,1)S(1)} collective-permute-done((bf16[256,4,128]{2,1,0:T(4,128)(2,1)S(1)}, bf16[256,4,128]{2,1,0:T(4,128)(2,1)S(1)}, u32[]{:S(2)}, u32[]{:S(2)}) %collective-permute-start.1) | collective-permute-done | bytes 262176 | tf_op jit(solution)/shard_map/ppermute | solution.py:21
  14.3 0.7 copy-done.20
  15.1 1.7 %pad_maximum_fusion.1 = bf16[256,16,128]{2,1,0:T(8,128)(2,1)S(1)} fusion(bf16[256,4,128]{2,1,0:T(4,128)(2,1)S(1)} %collective-permute-done.1, bf16[64,8,128]{2,1,0:T(8,128)(2,1)} %param.9, bf16[64,8,128]{2,1,0:T(8,128)(2,1)} %param.6, bf16[128,8,128]{2,1,0:T(8,128)(2,1)} %bitcast.52, bf16[256,4,128]{2,1,0:T(4,128)(2,1)S(1)} %collective-permute-done), kind=kLoop, calls=%fused_computation.11 | loop fusion | flops 5242880 | bytes 2097152 | tf_op jit(solution)/shard_map/concatenate | solution.py:22
  16.7 0.5 fusion.65
  17.2 0.9 copy.20
  18.2 0.9 copy.21
  19.1 1.3 collective-permute-start.3
  20.4 4.2 %collective-permute-start.2 = (bf16[256,16,4]{0,1,2:T(8,128)(2,1)S(1)}, bf16[256,16,4]{0,1,2:T(8,128)(2,1)S(1)}, u32[]{:S(2)}, u32[]{:S(2)}) collective-permute-start(bf16[256,16,4]{0,1,2:T(8,128)(2,1)S(1)} %copy.20), channel_id=1, source_target_pairs={{0,1},{1,2},{2,3},{3,4},{4,5},{5,6},{6,7},{7,8},{8,9},{9,10},{10,1... | collective-permute-start | bytes 98312 | tf_op jit(solution)/shard_map/ppermute | solution.py:20
  25.6 1.0 copy.22
  26.6 1.0 copy.23
  27.7 6.2 %pad_maximum_fusion = bf16[256,16,136]{2,1,0:T(8,128)(2,1)S(1)} fusion(bf16[256,16,4]{2,1,0:T(8,128)(2,1)S(1)} %copy.23, bf16[256,4,128]{2,1,0:T(4,128)(2,1)} %copy-done.20, bf16[64,8,128]{2,1,0:T(8,128)(2,1)S(1)} %copy-done.17, bf16[64,8,128]{2,1,0:T(8,128)(2,1)S(1)} %copy-done.18, bf16[128,8,128]{2,1,0:T(8,128)(2,1)S(1)} %bitcast.53, ...), kind=kLoop, calls=%fused_computation.8 | loop fusion | flops 7798784 | bytes 2228224 | tf_op jit(solution)/shard_map/concatenate | solution.py:22
  33.9 1.2 fusion.64
  35.1 0.7 slice.276
  35.7 1.7 %slice.298 = bf16[64,2176]{1,0:T(8,128)(2,1)S(1)} reshape(bf16[64,16,136]{2,1,0:T(8,128)(2,1)} %get-tuple-element.31) | data formatting | bytes 557056 | tf_op jit(solution)/shard_map/slice | solution.py:177
  37.5 1.7 %slice.287 = bf16[64,2176]{1,0:T(8,128)(2,1)S(1)} reshape(bf16[64,16,136]{2,1,0:T(8,128)(2,1)} %get-tuple-element.32) | data formatting | bytes 557056 | tf_op jit(solution)/shard_map/slice | solution.py:175
  39.2 1.4 reshape.135
  43.3 0.9 convolution_bitcast_fusion.2
  44.1 0.4 copy-done.9
  44.5 0.9 convolution_bitcast_fusion.1
  45.4 1.4 fusion.47
  48.0 0.9 convolution_bitcast_fusion
  50.1 0.9 convolution_bitcast_fusion.3
  51.2 0.4 fusion.59
  51.7 0.8 fusion.46
  52.9 2.1 %fusion.6 = f32[192,576]{1,0:T(8,128)} fusion(bf16[576,2176]{1,0:T(8,128)(2,1)S(1)} %slice_dynamic-update-slice_fusion.16, pred[2176]{0:T(1024)(128)(4,1)S(1)} %and.82, bf16[64,2176]{1,0:T(8,128)(2,1)S(1)} %get-tuple-element.28, bf16[64,2176]{1,0:T(8,128)(2,1)S(1)} %get-tuple-element.27, bf16[64,2176]{1,0:T(8,128)(2,1)S(1)} %fusion.23), kind=kOutput, calls=%fused_computation.23 | convolution fusion | flops 484220928 | bytes 3786880 | tf_op jit(solution)/shard_map/dot_general | solution.py:47
  55.0 1.9 %fusion.2 = f32[192,576]{1,0:T(8,128)} fusion(bf16[576,2176]{1,0:T(8,128)(2,1)S(1)} %slice_dynamic-update-slice_fusion.40, bf16[64,2176]{1,0:T(8,128)(2,1)S(1)} %get-tuple-element.18, pred[2176]{0:T(1024)(128)(4,1)S(1)} %and.82, bf16[64,2176]{1,0:T(8,128)(2,1)S(1)} %get-tuple-element.27, bf16[64,2176]{1,0:T(8,128)(2,1)S(1)} %fusion.23), kind=kOutput, calls=%fused_computation.18 | convolution fusion | flops 484220928 | bytes 3786880 | tf_op jit(solution)/shard_map/dot_general | solution.py:47
  56.9 3.2 %reshape.129 = bf16[64,16,136]{2,1,0:T(8,128)(2,1)} reshape(bf16[64,2176]{1,0:T(8,128)(2,1)} %fusion.46) | data formatting | bytes 557056 | tf_op jit(solution)/shard_map/reshape | solution.py:231
  60.1 1.8 %slice.363 = bf16[64,8,128]{2,1,0:T(8,128)(2,1)} slice(bf16[64,16,136]{2,1,0:T(8,128)(2,1)} %reshape.129), slice={[0:64], [4:12], [4:132]} | slice | bytes 262144 | tf_op jit(solution)/shard_map/slice | solution.py:231
  65.2 2.4 %fusion.58 = (bf16[64,2176]{1,0:T(8,128)(2,1)S(1)}, f32[64,2176]{1,0:T(8,128)S(1)}, bf16[64,2176]{1,0:T(8,128)(2,1)S(1)}, f32[64,2176]{1,0:T(8,128)}) fusion(f32[64,2176]{1,0:T(8,128)S(1)} %copy-done.15, f32[64,2176]{1,0:T(8,128)S(1)} %copy-done.11, bf16[64,2176]{1,0:T(8,128)(2,1)S(1)} %slice.298, bf16[64,1728]{1,0:T(8,128)(2,1)S(1)} %reshape.130, ...), kind=kOutput, calls=%fused_computation.158 | convolution fusion | flops 483246080 | bytes 11919360 | tf_op jit(solution)/shard_map/dot_general | solution.py:41
  67.6 1.4 %multiply_convert_fusion.1 = (bf16[64,2176]{1,0:T(8,128)(2,1)S(1)}, bf16[64,2176]{1,0:T(8,128)(2,1)S(1)}) fusion(f32[64,2176]{1,0:T(8,128)S(1)} %get-tuple-element.17, f32[192,2176]{1,0:T(8,128)S(1)} %convolution_bitcast_fusion.1, f32[192,2176]{1,0:T(8,128)} %copy-done.2), kind=kLoop, calls=%fused_computation.88 | loop fusion | flops 1531904 | bytes 2785280 | tf_op jit(solution)/shard_map/convert.8
  69.5 1.1 convolution_add_fusion
  70.6 0.6 copy-done.8
  71.3 1.1 convolution_add_fusion.1
  72.5 0.4 reshape.132
  72.9 1.0 pad.30
  73.9 53.5 %shard_map.84 = f32[16,16,7,128]{3,2,1,0:T(8,128)} custom-call(f32[16,112,128]{2,1,0:T(8,128)} %bitcast.47), custom_call_target="tpu_custom_call" | custom-call | tf_op jit(solution)/shard_map/pallas_call | solution.py:143
  127.3 1.3 reshape.134
  128.6 0.8 slice_multiply_fusion
  129.5 1.3 mul.142
  130.7 1.3 copy.26
  132.3 1.3 copy.25
  136.5 1.5 %fusion = f32[64,2176]{1,0:T(8,128)S(1)} fusion(bf16[64,1728]{1,0:T(8,128)(2,1)S(1)} %reshape.130, bf16[1728,2176]{1,0:T(8,128)(2,1)S(1)} %slice_dynamic-update-slice_fusion, f32[64,2176]{1,0:T(8,128)S(1)} %copy-done.16, f32[64,2176]{1,0:T(8,128)S(1)} %copy-done.12), kind=kOutput, calls=%fused_computation.5 | convolution fusion | flops 481574912 | bytes 9412608 | tf_op jit(solution)/shard_map/dot_general | solution.py:41
  137.9 1.4 reshape.131
  139.3 0.8 slice.365
  (116 shorter events, 13.7 us)
Async XLA Ops:
  0.6 42.4 %copy-start = (bf16[9,192,64]{1,2,0:T(8,128)(2,1)S(1)}, bf16[9,192,64]{1,2,0:T(8,128)(2,1)}, u32[]{:S(2)}) copy-start(bf16[9,192,64]{1,2,0:T(8,128)(2,1)} %param.7) | copy-start | bytes 663556
  2.0 7.8 %collective-permute-start = (bf16[256,4,128]{2,1,0:T(4,128)(2,1)S(1)}, bf16[256,4,128]{2,1,0:T(4,128)(2,1)S(1)}, u32[]{:S(2)}, u32[]{:S(2)}) collective-permute-start(bf16[256,4,128]{2,1,0:T(4,128)(2,1)S(1)} %get-tuple-element.38), channel_id=1, source_target_pairs={{0,16},{16,32},{32,48},{48,64},{64,80},{80,96},{96,112},{112,128},... | collective-permute-start | bytes 786440 | tf_op jit(solution)/shard_map/ppermute | solution.py:20
  6.5 7.8 %collective-permute-start.1 = (bf16[256,4,128]{2,1,0:T(4,128)(2,1)S(1)}, bf16[256,4,128]{2,1,0:T(4,128)(2,1)S(1)}, u32[]{:S(2)}, u32[]{:S(2)}) collective-permute-start(bf16[256,4,128]{2,1,0:T(4,128)(2,1)S(1)} %get-tuple-element.39), channel_id=1, source_target_pairs={{16,0},{32,16},{48,32},{64,48},{80,64},{96,80},{112,96},{128,112},... | collective-permute-start | bytes 786440 | tf_op jit(solution)/shard_map/ppermute | solution.py:21
  9.8 4.5 %copy-start.19 = (bf16[256,4,128]{2,1,0:T(4,128)(2,1)}, bf16[256,4,128]{2,1,0:T(4,128)(2,1)S(1)}, u32[]{:S(2)}) copy-start(bf16[256,4,128]{2,1,0:T(4,128)(2,1)S(1)} %collective-permute-done) | copy-start | bytes 786436
  14.3 0.7 copy-start.20
  16.7 8.2 %copy-start.13 = (bf16[9,192,64]{1,2,0:T(8,128)(2,1)S(1)}, bf16[9,192,64]{1,2,0:T(8,128)(2,1)}, u32[]{:S(2)}) copy-start(bf16[9,192,64]{1,2,0:T(8,128)(2,1)} %param.8) | copy-start | bytes 663556
  18.1 9.5 %copy-start.14 = (bf16[2,64,8,128]{3,2,1,0:T(8,128)(2,1)S(1)}, bf16[2,64,8,128]{3,2,1,0:T(8,128)(2,1)}, u32[]{:S(2)}) copy-start(bf16[2,64,8,128]{3,2,1,0:T(8,128)(2,1)} %param.5) | copy-start | bytes 786436
  18.1 9.5 %copy-start.17 = (bf16[64,8,128]{2,1,0:T(8,128)(2,1)S(1)}, bf16[64,8,128]{2,1,0:T(8,128)(2,1)}, u32[]{:S(2)}) copy-start(bf16[64,8,128]{2,1,0:T(8,128)(2,1)} %param.9) | copy-start | bytes 393220
  18.2 9.5 %copy-start.18 = (bf16[64,8,128]{2,1,0:T(8,128)(2,1)S(1)}, bf16[64,8,128]{2,1,0:T(8,128)(2,1)}, u32[]{:S(2)}) copy-start(bf16[64,8,128]{2,1,0:T(8,128)(2,1)} %param.6) | copy-start | bytes 393220
  19.1 7.5 %collective-permute-start.3 = (bf16[256,16,4]{0,1,2:T(8,128)(2,1)S(1)}, bf16[256,16,4]{0,1,2:T(8,128)(2,1)S(1)}, u32[]{:S(2)}, u32[]{:S(2)}) collective-permute-start(bf16[256,16,4]{0,1,2:T(8,128)(2,1)S(1)} %copy.21), channel_id=1, source_target_pairs={{1,0},{2,1},{3,2},{4,3},{5,4},{6,5},{7,6},{8,7},{9,8},{10,9},{11,1... | collective-permute-start | bytes 98312 | tf_op jit(solution)/shard_map/ppermute | solution.py:21
  20.4 5.2 %collective-permute-start.2 = (bf16[256,16,4]{0,1,2:T(8,128)(2,1)S(1)}, bf16[256,16,4]{0,1,2:T(8,128)(2,1)S(1)}, u32[]{:S(2)}, u32[]{:S(2)}) collective-permute-start(bf16[256,16,4]{0,1,2:T(8,128)(2,1)S(1)} %copy.20), channel_id=1, source_target_pairs={{0,1},{1,2},{2,3},{3,4},{4,5},{5,6},{6,7},{7,8},{8,9},{9,10},{10,1... | collective-permute-start | bytes 98312 | tf_op jit(solution)/shard_map/ppermute | solution.py:20
  41.8 1.5 %copy-start.7 = (bf16[576,2176]{1,0:T(8,128)(2,1)}, bf16[576,2176]{1,0:T(8,128)(2,1)S(1)}, u32[]{:S(2)}) copy-start(bf16[576,2176]{1,0:T(8,128)(2,1)S(1)} %slice_dynamic-update-slice_fusion.32) | copy-start | bytes 7520260
  43.0 1.5 %copy-start.9 = (bf16[576,2176]{1,0:T(8,128)(2,1)}, bf16[576,2176]{1,0:T(8,128)(2,1)S(1)}, u32[]{:S(2)}) copy-start(bf16[576,2176]{1,0:T(8,128)(2,1)S(1)} %slice_dynamic-update-slice_fusion.24) | copy-start | bytes 7520260
  44.1 1.3 copy-start.2
  50.1 1.1 copy-start.3
  51.6 1.2 copy-start.5
  63.7 1.1 copy-start.4
  63.7 1.2 copy-start.6
  63.7 1.4 copy-start.11
  63.7 1.5 %copy-start.15 = (f32[64,2176]{1,0:T(8,128)S(1)}, f32[64,2176]{1,0:T(8,128)}, u32[]{:S(2)}) copy-start(f32[64,2176]{1,0:T(8,128)} %get-tuple-element.23) | copy-start | bytes 1671172
  67.6 1.9 %copy-start.10 = (bf16[576,2176]{1,0:T(8,128)(2,1)S(1)}, bf16[576,2176]{1,0:T(8,128)(2,1)}, u32[]{:S(2)}) copy-start(bf16[576,2176]{1,0:T(8,128)(2,1)} %copy-done.9) | copy-start | bytes 7520260
  67.6 1.9 %copy-start.22 = (f32[192,576]{1,0:T(8,128)S(1)}, f32[192,576]{1,0:T(8,128)}, u32[]{:S(2)}) copy-start(f32[192,576]{1,0:T(8,128)} %fusion.6) | copy-start | bytes 1327108
  69.5 1.7 %copy-start.8 = (bf16[576,2176]{1,0:T(8,128)(2,1)S(1)}, bf16[576,2176]{1,0:T(8,128)(2,1)}, u32[]{:S(2)}) copy-start(bf16[576,2176]{1,0:T(8,128)(2,1)} %copy-done.7) | copy-start | bytes 7520260
  69.5 1.8 %copy-start.21 = (f32[192,576]{1,0:T(8,128)S(1)}, f32[192,576]{1,0:T(8,128)}, u32[]{:S(2)}) copy-start(f32[192,576]{1,0:T(8,128)} %fusion.2) | copy-start | bytes 1327108
  135.3 1.1 copy-start.12
  135.3 1.2 copy-start.16
  136.5 3.7 %copy-start.1 = (bf16[9,192,64]{1,2,0:T(8,128)(2,1)S(1)}, bf16[9,192,64]{1,2,0:T(8,128)(2,1)}, u32[]{:S(2)}) copy-start(bf16[9,192,64]{1,2,0:T(8,128)(2,1)} %param.7) | copy-start | bytes 663556
